TPU v7x, 32 devices: a whole 2x2x4 slice. The times are simulated.
32 devices in a mesh: blk: 8 (over z, x), grp: 4 (over y, core).
Axes of the slice: x: 2, y: 2, z: 4, core: 2. Of those that a mesh axis runs over, the one named last changes fastest.
Arguments:
- queries: bfloat16 [16384, 512], P(('blk', 'grp')), may hold values from -64 to 64
- keys: bfloat16 [16384, 128], P(('blk', 'grp')), may hold values from -8 to 8
- values: bfloat16 [16384, 128], P(('blk', 'grp')), may hold values from -6 to 6
- selected: int32 [32, 16], replicated, may hold values from 0 to 255, as said below
- key_in: bfloat16 [4096, 256], replicated, may hold values from -0.09375 to 0.09375
- key_out: bfloat16 [256, 128], replicated, may hold values from -0.375 to 0.375
- value_in: bfloat16 [4096, 256], replicated, may hold values from -0.09375 to 0.09375
- value_out: bfloat16 [256, 128], replicated, may hold values from -0.375 to 0.375
- positions: bfloat16 [2, 32, 128], replicated, may hold values from -5 to 5
- gate_weight: bfloat16 [512, 12], replicated, may hold values from -0.25 to 0.25
Outputs:
- attended: bfloat16 [16384, 512], P(('blk', 'grp'))
Inputs may be any that keep to these rules, and one draw needn't show every extreme that they name: `selected`: row d lists 16 different fine blocks. Write r = 32 and b = d // 4. Entry 0 is the first fine block of group d's own tokens. Every listed block j with j // r different from b has j // r < b, and no two listed blocks share a value of j // r other than b. Blocks with j // r == b may lie after group d's tokens.
All inputs are finite; a program needn't handle non-finite values.
Results may differ from a plain program's by a relative error of at most 0.004.
Values may be sent and summed in bfloat16 or wider, within the bound.
A program may use at most 64 MiB of HBM per device.

v0:
```python
import jax
import jax.numpy as jnp
from jax import lax
from jax.sharding import PartitionSpec as P

HEAD_DIM = 128
HEADS = 4
CMP_BLOCK = 32
SEL_BLOCK = 64
TOPN = 16
WINDOW = 512
NEG = -1e30


def from_behind(block, axis, distance):
    devices = range(lax.axis_size(axis))
    route = [(i - distance, i) for i in devices if i - distance in devices]
    return lax.ppermute(block, axis, route)


def compress(tokens, shift, w_in, w_out):
    count = tokens.shape[0] // CMP_BLOCK
    mixed = (
        tokens.astype(jnp.float32).reshape(count, CMP_BLOCK, HEAD_DIM)
        + shift.astype(jnp.float32)[None]
    )
    flat = mixed.astype(jnp.bfloat16).reshape(count, CMP_BLOCK * HEAD_DIM)
    hidden = jax.nn.silu(jnp.dot(flat, w_in, preferred_element_type=jnp.float32)).astype(
        jnp.bfloat16
    )
    return jnp.dot(hidden, w_out, preferred_element_type=jnp.float32).astype(jnp.bfloat16)


def attend(query_rows, query_pos, key_rows, value_rows, key_pos, span):
    scale = HEAD_DIM ** (-0.5)
    scores = (
        jnp.einsum("qhd,kd->qhk", query_rows, key_rows, preferred_element_type=jnp.float32) * scale
    )
    allowed = (
        (key_pos[None, :] <= query_pos[:, None])
        & (key_pos[None, :] > query_pos[:, None] - span)
        & (key_pos[None, :] >= 0)
    )
    scores = jnp.where(allowed[:, None, :], scores, NEG)
    top = jnp.max(scores, axis=2, keepdims=True)
    weights = jnp.exp(scores - top)
    total = jnp.sum(weights, axis=2)
    mixed = jnp.einsum(
        "qhk,kd->qhd", weights.astype(jnp.bfloat16), value_rows, preferred_element_type=jnp.float32
    )
    return mixed / total[..., None]


def make_fold(query_heads, query_pos):
    scale = HEAD_DIM ** (-0.5)
    toks = query_heads.shape[0]

    def fold(carry, piece, start):
        best, total, accum = carry
        piece_keys, piece_values = piece
        count = piece_keys.shape[0]
        key_end = jnp.arange(count, dtype=jnp.int32) * CMP_BLOCK + (CMP_BLOCK - 1)
        block_rows = toks
        while (
            block_rows > 32 and block_rows % 2 == 0 and (HEADS * block_rows * count * 4 > 1 << 24)
        ):
            block_rows = block_rows // 2
        steps = toks // block_rows

        def one(items):
            rows, pos, old_best, old_total, old_accum = items
            scores = (
                jnp.einsum("qhd,kd->qhk", rows, piece_keys, preferred_element_type=jnp.float32)
                * scale
            )
            scores = jnp.where((key_end[None, :] <= pos[:, None])[:, None, :], scores, NEG)
            new_best = jnp.maximum(old_best, jnp.max(scores, axis=2))
            weights = jnp.exp(scores - new_best[..., None])
            factor = jnp.exp(old_best - new_best)
            new_total = old_total * factor + jnp.sum(weights, axis=2)
            product = jnp.einsum(
                "qhk,kd->qhd",
                weights.astype(jnp.bfloat16),
                piece_values,
                preferred_element_type=jnp.float32,
            )
            return (new_best, new_total, old_accum * factor[..., None] + product)

        items = (
            query_heads.reshape(steps, block_rows, HEADS, HEAD_DIM),
            query_pos.reshape(steps, block_rows),
            best.reshape(steps, block_rows, HEADS),
            total.reshape(steps, block_rows, HEADS),
            accum.reshape(steps, block_rows, HEADS, HEAD_DIM),
        )
        new_best, new_total, new_accum = lax.map(one, items)
        return (
            new_best.reshape(toks, HEADS),
            new_total.reshape(toks, HEADS),
            new_accum.reshape(toks, HEADS, HEAD_DIM),
        )

    return fold


def per_device(
    queries, keys, values, selected, key_in, key_out, value_in, value_out, positions, gate_weight
):
    stretches = lax.axis_size("blk")
    group_size = lax.axis_size("grp")
    stretch = lax.axis_index("blk")
    column = lax.axis_index("grp")
    toks = queries.shape[0]
    seq_len = stretches * group_size * toks
    position = stretch * group_size + column
    query_pos = position * toks + jnp.arange(toks, dtype=jnp.int32)
    query_heads = queries.reshape(toks, HEADS, HEAD_DIM)
    row_keys, row_values = (
        lax.all_gather(keys, "grp", axis=0, tiled=True),
        lax.all_gather(values, "grp", axis=0, tiled=True),
    )
    fold = make_fold(query_heads, query_pos)
    start_state = (
        jnp.zeros((toks, HEADS), jnp.float32),
        jnp.ones((toks, HEADS), jnp.float32),
        jnp.zeros((toks, HEADS, HEAD_DIM), jnp.float32),
    )
    packed = (
        compress(row_keys, positions[0], key_in, key_out),
        compress(row_values, positions[1], value_in, value_out),
    )
    best, total, accum = fold(
        start_state,
        (
            lax.all_gather(packed[0], "blk", axis=0, tiled=True),
            lax.all_gather(packed[1], "blk", axis=0, tiled=True),
        ),
        jnp.int32(0),
    )
    coarse = accum / total[..., None]
    per_row = group_size * toks // SEL_BLOCK
    row_blocks = jnp.concatenate([row_keys, row_values], axis=1).reshape(
        per_row, SEL_BLOCK, 2 * HEAD_DIM
    )
    requests = jnp.take(selected.reshape(stretches, group_size, TOPN), column, axis=1)
    targets = jnp.arange(stretches, dtype=jnp.int32)
    match = (requests // per_row == stretch) & (targets[:, None] != stretch)
    picked = jnp.sum(jnp.where(match, requests % per_row, 0), axis=1)
    outgoing = jnp.take(row_blocks, picked, axis=0)
    incoming = lax.all_to_all(outgoing, "blk", split_axis=0, concat_axis=0, tiled=True)
    mine = lax.dynamic_index_in_dim(selected, position, 0, keepdims=False)
    owners = mine // per_row
    nearby = jnp.take(row_blocks, mine % per_row, axis=0)
    remote = jnp.take(incoming, owners, axis=0)
    fine_rows = jnp.where((owners == stretch)[:, None, None], nearby, remote).reshape(
        TOPN * SEL_BLOCK, 2 * HEAD_DIM
    )
    fine_keys = fine_rows[:, :HEAD_DIM]
    fine_values = fine_rows[:, HEAD_DIM:]
    fine_pos = (
        mine[:, None] * SEL_BLOCK + jnp.arange(SEL_BLOCK, dtype=jnp.int32)[None, :]
    ).reshape(-1)
    reach = (WINDOW + toks - 1) // toks
    moved_keys, moved_values = from_behind((keys, values), ("blk", "grp"), 1)
    key_parts = [moved_keys]
    value_parts = [moved_values]
    wide_keys = jnp.concatenate(key_parts + [keys], axis=0)
    wide_values = jnp.concatenate(value_parts + [values], axis=0)
    wide_pos = position * toks - reach * toks + jnp.arange((reach + 1) * toks, dtype=jnp.int32)
    block_rows = min(toks, 128)
    steps = toks // block_rows

    def both_blocks(index):
        first = index * block_rows
        rows = lax.dynamic_slice_in_dim(query_heads, first, block_rows, 0)
        pos = lax.dynamic_slice_in_dim(query_pos, first, block_rows, 0)
        fine_part = attend(rows, pos, fine_keys, fine_values, fine_pos, seq_len + 1)
        key_start = reach * toks + first - WINDOW
        near_keys = lax.dynamic_slice_in_dim(wide_keys, key_start, block_rows + WINDOW, 0)
        near_values = lax.dynamic_slice_in_dim(wide_values, key_start, block_rows + WINDOW, 0)
        near_pos = lax.dynamic_slice_in_dim(wide_pos, key_start, block_rows + WINDOW, 0)
        local_part = attend(rows, pos, near_keys, near_values, near_pos, WINDOW)
        return (fine_part, local_part)

    fine, local = lax.map(both_blocks, jnp.arange(steps, dtype=jnp.int32))
    fine = fine.reshape(toks, HEADS, HEAD_DIM)
    local = local.reshape(toks, HEADS, HEAD_DIM)
    gates = jax.nn.sigmoid(
        jnp.dot(queries, gate_weight, preferred_element_type=jnp.float32)
    ).reshape(toks, 3, HEADS)
    mixed = (
        gates[:, 0, :, None] * coarse + gates[:, 1, :, None] * fine + gates[:, 2, :, None] * local
    )
    return mixed.astype(jnp.bfloat16).reshape(toks, HEADS * HEAD_DIM)


def solution(mesh):
    return jax.shard_map(
        per_device,
        mesh=mesh,
        in_specs=(
            P(("blk", "grp"), None),
            P(("blk", "grp"), None),
            P(("blk", "grp"), None),
            P(),
            P(),
            P(),
            P(),
            P(),
            P(),
            P(),
        ),
        out_specs=P(("blk", "grp"), None),
        check_vma=False,
    )
```

profile of v0, /device:TPU:0, one launch (start us, length us, event | category | flops | bytes accessed | tf_op | source)
XLA Modules:
  0.0 162.3 jit_solution(4513411098601739997)
XLA Ops:
  0.0 3.2 %collective-permute-start = (bf16[512,128]{1,0:T(8,128)(2,1)}, bf16[512,128]{1,0:T(8,128)(2,1)}, u32[]{:S(2)}, u32[]{:S(2)}) collective-permute-start(bf16[512,128]{1,0:T(8,128)(2,1)} %param.13), channel_id=1, source_target_pairs={{0,1},{1,2},{2,3},{3,4},{4,5},{5,6},{6,7},{7,8},{8,9},{9,10},{10,1... | collective-permute-start | bytes 393224 | tf_op jit(solution)/shard_map/ppermute | solution.py:18
  3.2 4.5 %collective-permute-start.1 = (bf16[512,128]{1,0:T(8,128)(2,1)}, bf16[512,128]{1,0:T(8,128)(2,1)}, u32[]{:S(2)}, u32[]{:S(2)}) collective-permute-start(bf16[512,128]{1,0:T(8,128)(2,1)} %param.14), channel_id=1, source_target_pairs={{0,1},{1,2},{2,3},{3,4},{4,5},{5,6},{6,7},{7,8},{8,9},{9,10},{10,1... | collective-permute-start | bytes 393224 | tf_op jit(solution)/shard_map/ppermute | solution.py:18
  7.7 6.7 %all_gather.12 = bf16[2048,128]{1,0:T(8,128)(2,1)S(1)} all-gather(bf16[512,128]{1,0:T(8,128)(2,1)} %param.13), channel_id=1, replica_groups=mesh['blk'=8,'grp'=4] {'grp'}, dimensions={0}, use_global_device_ids=true | all-gather | bytes 655360 | tf_op jit(solution)/shard_map/all_gather | solution.py:119
  14.4 7.5 %all_gather.14 = bf16[2048,128]{1,0:T(8,128)(2,1)S(1)} all-gather(bf16[512,128]{1,0:T(8,128)(2,1)} %param.14), channel_id=1, replica_groups=mesh['blk'=8,'grp'=4] {'grp'}, dimensions={0}, use_global_device_ids=true | all-gather | bytes 655360 | tf_op jit(solution)/shard_map/all_gather | solution.py:120
  22.9 1.1 pad_maximum_fusion
  24.0 1.8 %gather_fusion.1 = bf16[8,64,256]{2,1,0:T(8,128)(2,1)S(1)} fusion(bf16[32,64,256]{2,1,0:T(8,128)(2,1)} %bitcast.141, s32[1024]{0:T(1024)S(1)} %pad_clamp_fusion.1), kind=kCustom, calls=%fused_computation.1 | custom fusion | bytes 524320 | tf_op jit(solution)/shard_map/jit(_take)/gather | solution.py:149
  26.6 6.0 %all-to-all-start = ((bf16[8,64,256]{2,1,0:T(8,128)(2,1)}), bf16[8,64,256]{2,1,0:T(8,128)(2,1)S(1)}, u32[]{:S(2)}, u32[]{:S(2)}) async-start(bf16[8,64,256]{2,1,0:T(8,128)(2,1)} %broadcast_select_fusion), calls=%async_computation | async-start | bytes 524288 | tf_op jit(solution)/shard_map/all_to_all | solution.py:150
  33.2 1.2 reshape.482
  34.4 1.2 reshape.485
  38.1 1.8 %convolution_convert_fusion.1 = bf16[64,128]{1,0:T(8,128)(2,1)S(1)} fusion(bf16[256,128]{1,0:T(8,128)(2,1)S(1)} %copy-done.9, bf16[4096,256]{1,0:T(8,128)(2,1)S(1)} %copy-done, f32[64,4096]{1,0:T(8,128)} %reshape.482, f32[4096]{0:T(1024)S(1)} %get-tuple-element.393), kind=kOutput, calls=%fused_computation.58 | convolution fusion | flops 139026432 | bytes 3244032 | tf_op jit(solution)/shard_map/dot_general | solution.py:31
  39.9 31.1 %all_gather.13 = bf16[512,128]{1,0:T(8,128)(2,1)S(1)} all-gather(bf16[64,128]{1,0:T(8,128)(2,1)S(1)} %convolution_convert_fusion.1), channel_id=1, replica_groups=mesh['blk'=8,'grp'=4] {'blk'}, dimensions={0}, use_global_device_ids=true | all-gather | bytes 147456 | tf_op jit(solution)/shard_map/all_gather | solution.py:135
  71.2 0.9 broadcast_compare_fusion.2
  73.0 0.9 fusion.30
  73.9 1.0 copy-done.1
  74.9 2.5 %convolution_convert_fusion = bf16[64,128]{1,0:T(8,128)(2,1)S(1)} fusion(bf16[256,128]{1,0:T(8,128)(2,1)S(1)} %copy-done.10, bf16[4096,256]{1,0:T(8,128)(2,1)} %param.18, f32[64,4096]{1,0:T(8,128)} %reshape.485, f32[4096]{0:T(1024)S(1)} %get-tuple-element.392), kind=kOutput, calls=%fused_computation.57 | convolution fusion | flops 139026432 | bytes 3244032 | tf_op jit(solution)/shard_map/dot_general | solution.py:31
  77.4 30.7 %all_gather.15 = bf16[512,128]{1,0:T(8,128)(2,1)S(1)} all-gather(bf16[64,128]{1,0:T(8,128)(2,1)S(1)} %convolution_convert_fusion), channel_id=1, replica_groups=mesh['blk'=8,'grp'=4] {'blk'}, dimensions={0}, use_global_device_ids=true | all-gather | bytes 147456 | tf_op jit(solution)/shard_map/all_gather | solution.py:136
  108.1 1.3 fusion.41
  109.5 4.3 %divide_multiply_fusion = f32[512,4,128]{0,2,1:T(8,128)} fusion(f32[512,512,4]{1,0,2:T(8,128)} %copy-done.1, f32[512,4]{0,1:T(4,128)S(1)} %broadcast_maximum_fusion, pred[512,512]{0,1:T(8,128)(4,1)S(1)} %broadcast_compare_fusion.2, f32[512,4]{0,1:T(4,128)S(1)} %get-tuple-element.395, f32[512,4]{0,1:T(4,128)S(1)} %get-tuple-element.394, ...), kind=kOutput, calls=%fused_computation.65 | convolution fusion | flops 273416192 | bytes 5668864 | tf_op jit(solution)/shard_map/while/body/eval_jaxpr/qhk,kd->qhd/dot_general | solution.py:81
  113.9 2.6 %copy.24 = f32[512,512]{1,0:T(8,128)} copy(f32[512,512]{0,1:T(8,128)} %bitcast.143) | data formatting | bytes 2097152 | tf_op jit(solution)/shard_map/mul | solution.py:192
  116.5 2.6 %gather_fusion = bf16[16,64,256]{2,1,0:T(8,128)(2,1)} fusion(bf16[32,64,256]{2,1,0:T(8,128)(2,1)} %bitcast.142, s32[1024]{0:T(1024)S(1)} %get-tuple-element.402), kind=kCustom, calls=%fused_computation | custom fusion | bytes 1048640 | tf_op jit(solution)/shard_map/jit(_take)/gather | solution.py:153
  121.4 0.9 pad_maximum_fusion.1
  122.3 1.6 %pad_maximum_fusion.2 = bf16[1024,128]{1,0:T(8,128)(2,1)} fusion(bf16[512,128]{1,0:T(8,128)(2,1)S(1)} %copy-done.6, bf16[512,128]{1,0:T(8,128)(2,1)} %collective-permute-done.1), kind=kLoop, calls=%fused_computation.77 | loop fusion | flops 524288 | bytes 524288 | tf_op jit(solution)/shard_map/concatenate | solution.py:168
  124.0 1.4 gather_fusion.2
  125.3 1.9 %fusion.49 = bf16[1024,256]{1,0:T(8,128)(2,1)S(1)} fusion(bf16[16,64,256]{2,1,0:T(8,128)(2,1)} %gather_fusion.2, bf16[16,64,256]{2,1,0:T(8,128)(2,1)} %gather_fusion, pred[1024]{0:T(1024)(128)(4,1)S(1)} %broadcast_in_dim.198, pred[1024]{0:T(1024)(128)(4,1)S(1)} %broadcast_in_dim.194, pred[1024]{0:T(1024)(128)(4,1)S(1)} %broadcast_in_dim.191), kind=kLoop, calls=%fused_computation.71 | loop fusion | flops 786432 | bytes 1575936 | tf_op jit(solution)/shard_map/jit(_where)/select_n | solution.py:155
  127.9 28.5 %while.24 = (s32[]{:T(128)}, f32[4,128,4,128]{3,2,1,0:T(4,128)}, f32[4,128,4,128]{3,2,1,0:T(4,128)}, s32[4]{0:T(128)S(1)}, s32[512]{0:T(512)}, /*index=5*/bf16[5...) while((s32[]{:T(128)}, f32[4,128,4,128]{3,2,1,0:T(4,128)}, ...), condition=%wide.region_8.9_spmd.clone, body=%wide.region_3.8_spmd.clone.sunk | while | flops 445252480 | bytes 15753344 | solution.py:185
  133.9 1.2 copy_dynamic-update-slice_fusion.3
  141.0 1.1 copy_dynamic-update-slice_fusion.3
  148.2 1.2 copy_dynamic-update-slice_fusion.3
  155.3 1.1 copy_dynamic-update-slice_fusion.3
  156.5 1.7 %mul.142 = f32[512,4,128]{2,1,0:T(4,128)S(1)} broadcast(f32[512,4]{1,0:T(8,128)} %copy.20), dimensions={0,1} | broadcast | bytes 1056768 | tf_op jit(solution)/shard_map/mul | solution.py:192
  158.2 1.6 mul.147
  159.7 2.5 %fusion.43 = bf16[512,512]{1,0:T(8,128)(2,1)} fusion(f32[64,8,4,128]{3,2,1,0:T(4,128)} %bitcast.145, f32[64,8,4,128]{3,2,1,0:T(4,128)S(1)} %bitcast.140, f32[512,512]{1,0:T(8,128)S(1)} %copy-done.2, f32[64,8,4,128]{3,2,1,0:T(4,128)S(1)} %bitcast.144, f32[64,8,4,128]{3,2,1,0:T(4,128)S(1)} %bitcast.139), kind=kLoop, calls=%fused_computation.61 | loop fusion | flops 1310720 | bytes 5767168 | tf_op jit(solution)/shard_map/convert_element_type | solution.py:194
  (150 shorter events, 29.8 us)
Async XLA Ops:
  0.0 38.1 %copy-start = (bf16[4096,256]{1,0:T(8,128)(2,1)S(1)}, bf16[4096,256]{1,0:T(8,128)(2,1)}, u32[]{:S(2)}) copy-start(bf16[4096,256]{1,0:T(8,128)(2,1)} %param.16) | copy-start | bytes 6291460
  0.0 121.4 %collective-permute-start = (bf16[512,128]{1,0:T(8,128)(2,1)}, bf16[512,128]{1,0:T(8,128)(2,1)}, u32[]{:S(2)}, u32[]{:S(2)}) collective-permute-start(bf16[512,128]{1,0:T(8,128)(2,1)} %param.13), channel_id=1, source_target_pairs={{0,1},{1,2},{2,3},{3,4},{4,5},{5,6},{6,7},{7,8},{8,9},{9,10},{10,1... | collective-permute-start | bytes 393224 | tf_op jit(solution)/shard_map/ppermute | solution.py:18
  3.2 119.1 %collective-permute-start.1 = (bf16[512,128]{1,0:T(8,128)(2,1)}, bf16[512,128]{1,0:T(8,128)(2,1)}, u32[]{:S(2)}, u32[]{:S(2)}) collective-permute-start(bf16[512,128]{1,0:T(8,128)(2,1)} %param.14), channel_id=1, source_target_pairs={{0,1},{1,2},{2,3},{3,4},{4,5},{5,6},{6,7},{7,8},{8,9},{9,10},{10,1... | collective-permute-start | bytes 393224 | tf_op jit(solution)/shard_map/ppermute | solution.py:18
  25.8 9.8 %copy-start.11 = (s32[32,16]{0,1:T(8,128)S(1)}, s32[32,16]{0,1:T(8,128)}, u32[]{:S(2)}) copy-start(s32[32,16]{0,1:T(8,128)} %param.15) | copy-start | bytes 6148
  25.8 12.3 %copy-start.12 = (bf16[2,32,128]{2,1,0:T(8,128)(2,1)S(1)}, bf16[2,32,128]{2,1,0:T(8,128)(2,1)}, u32[]{:S(2)}) copy-start(bf16[2,32,128]{2,1,0:T(8,128)(2,1)} %param.20) | copy-start | bytes 49156
  25.8 12.3 %copy-start.9 = (bf16[256,128]{1,0:T(8,128)(2,1)S(1)}, bf16[256,128]{1,0:T(8,128)(2,1)}, u32[]{:S(2)}) copy-start(bf16[256,128]{1,0:T(8,128)(2,1)} %param.17) | copy-start | bytes 196612
  26.6 97.4 %all-to-all-start = ((bf16[8,64,256]{2,1,0:T(8,128)(2,1)}), bf16[8,64,256]{2,1,0:T(8,128)(2,1)S(1)}, u32[]{:S(2)}, u32[]{:S(2)}) async-start(bf16[8,64,256]{2,1,0:T(8,128)(2,1)} %broadcast_select_fusion), calls=%async_computation | async-start | bytes 524288 | tf_op jit(solution)/shard_map/all_to_all | solution.py:150
  35.6 35.4 %copy-start.3 = (bf16[512,512]{1,0:T(8,128)(2,1)S(1)}, bf16[512,512]{1,0:T(8,128)(2,1)}, u32[]{:S(2)}) copy-start(bf16[512,512]{1,0:T(8,128)(2,1)} %param.12) | copy-start | bytes 1572868
  73.0 1.9 %copy-start.1 = (f32[512,512,4]{1,0,2:T(8,128)}, f32[512,512,4]{1,0,2:T(8,128)S(1)}, u32[]{:S(2)}) copy-start(f32[512,512,4]{1,0,2:T(8,128)S(1)} %get-tuple-element.400) | copy-start | bytes 12582916
  73.0 1.9 %copy-start.10 = (bf16[256,128]{1,0:T(8,128)(2,1)S(1)}, bf16[256,128]{1,0:T(8,128)(2,1)}, u32[]{:S(2)}) copy-start(bf16[256,128]{1,0:T(8,128)(2,1)} %param.19) | copy-start | bytes 196612
  74.9 33.2 %copy-start.13 = (bf16[512,12]{0,1:T(8,128)(2,1)S(1)}, bf16[512,12]{0,1:T(8,128)(2,1)}, u32[]{:S(2)}) copy-start(bf16[512,12]{0,1:T(8,128)(2,1)} %param.21) | copy-start | bytes 36868
  74.9 34.6 %copy-start.19 = (s32[16]{0:T(128)S(1)}, s32[16]{0:T(128)}, u32[]{:S(2)}) copy-start(s32[16]{0:T(128)} %get-tuple-element.380) | copy-start | bytes 196
  109.5 4.4 %copy-start.17 = (s32[16]{0:T(128)S(1)}, s32[16]{0:T(128)}, u32[]{:S(2)}) copy-start(s32[16]{0:T(128)} %get-tuple-element.397) | copy-start | bytes 196
  109.5 4.4 %copy-start.18 = (s32[16]{0:T(128)S(1)}, s32[16]{0:T(128)}, u32[]{:S(2)}) copy-start(s32[16]{0:T(128)} %get-tuple-element.398) | copy-start | bytes 196
  113.9 5.4 %copy-start.16 = (pred[16]{0:T(512)(128)(4,1)S(1)}, pred[16]{0:T(512)(128)(4,1)}, u32[]{:S(2)}) copy-start(pred[16]{0:T(512)(128)(4,1)} %get-tuple-element.379) | copy-start | bytes 52
  113.9 5.6 %copy-start.15 = (pred[16]{0:T(512)(128)(4,1)S(1)}, pred[16]{0:T(512)(128)(4,1)}, u32[]{:S(2)}) copy-start(pred[16]{0:T(512)(128)(4,1)} %get-tuple-element.396) | copy-start | bytes 52
  113.9 7.5 %copy-start.5 = (bf16[512,128]{1,0:T(8,128)(2,1)S(1)}, bf16[512,128]{1,0:T(8,128)(2,1)}, u32[]{:S(2)}) copy-start(bf16[512,128]{1,0:T(8,128)(2,1)} %param.13) | copy-start | bytes 393220
  113.9 8.4 %copy-start.6 = (bf16[512,128]{1,0:T(8,128)(2,1)S(1)}, bf16[512,128]{1,0:T(8,128)(2,1)}, u32[]{:S(2)}) copy-start(bf16[512,128]{1,0:T(8,128)(2,1)} %param.14) | copy-start | bytes 393220
  122.3 5.6 %copy-start.14 = (s32[16]{0:T(128)S(1)}, s32[16]{0:T(128)}, u32[]{:S(2)}) copy-start(s32[16]{0:T(128)} %broadcast_multiply_fusion) | copy-start | bytes 196
  130.4 1.2 copy-start.8
  132.3 1.1 copy-start.7
  137.5 1.2 copy-start.8
  139.5 1.1 copy-start.7
  144.7 1.2 copy-start.8
  146.6 1.1 copy-start.7
  151.8 1.2 copy-start.8
  153.7 1.1 copy-start.7
  156.5 3.3 %copy-start.2 = (f32[512,512]{1,0:T(8,128)S(1)}, f32[512,512]{1,0:T(8,128)}, u32[]{:S(2)}) copy-start(f32[512,512]{1,0:T(8,128)} %copy.24) | copy-start | bytes 3145732
  156.5 3.3 %copy-start.4 = (f32[4,128,4,128]{3,2,1,0:T(4,128)S(1)}, f32[4,128,4,128]{3,2,1,0:T(4,128)}, u32[]{:S(2)}) copy-start(f32[4,128,4,128]{3,2,1,0:T(4,128)} %get-tuple-element.299) | copy-start | bytes 3145732
where the time goes:
time: 163 us; the launch traced here: 162 us
  blocking collectives  76 us (47%)
  local copies, waits for them, and re-layouts  26.9 us (17%)
  other arithmetic  22.7 us (14%)
  matrix products  19.6 us (12%)
  starting transfers between devices  13.7 us (8%)
  loops' own time  3.12 us (2%)
    all_gather x1, blocking collectives, per_device(): lax.all_gather(packed[0], 'blk', axis=0, tiled=True)  31.1 us
    all_gather x1, blocking collectives, per_device(): lax.all_gather(packed[1], 'blk', axis=0, tiled=True)  30.7 us
    ppermute x2, starting transfers between devices, from_behind(): return lax.ppermute(block, axis, route)  7.7 us
    all_gather x1, blocking collectives, per_device(): lax.all_gather(values, 'grp', axis=0, tiled=True)  7.48 us
    all_gather x1, blocking collectives, per_device(): lax.all_gather(keys, 'grp', axis=0, tiled=True)  6.7 us
    all_to_all x1, starting transfers between devices, per_device(): lax.all_to_all(outgoing, 'blk', split_axis=0, concat_axis=0, tiled=True)  6 us
    dynamic_update_slice x4, local copies, waits for them, and re-layouts, per_device(): fine, local = lax.map(both_blocks, jnp.arange(steps, dtype=jnp.int32))  4.64 us
    dot_general x8, matrix products, attend(): jnp.einsum('qhd,kd->qhk', query_rows, key_rows, preferred_element_type=jn...  4.55 us
  transfers between devices with their start and end apart: 3, of which 0 were waited for; matrix products, arithmetic and copies ran while one was open for 20% of the time, Pallas kernels for 0%

commit v1 on v0

--- a/solution.py
+++ b/solution.py
@@ -133,7 +133,9 @@
         start_state,
         (
             lax.all_gather(packed[0], "blk", axis=0, tiled=True),
-            lax.all_gather(packed[1], "blk", axis=0, tiled=True),
+            jnp.concatenate(
+                lax.all_to_all(jnp.stack([packed[1]] * lax.axis_size("blk")), "blk", 0, 0), axis=0
+            ),
         ),
         jnp.int32(0),
     )

time: 163 us -> 145 us (0.89)
  blocking collectives: 76 us -> 49.3 us
  local copies, waits for them, and re-layouts: 26.9 us -> 32.4 us
  starting transfers between devices: 13.7 us -> 16.5 us
    all_gather x1 -> x0, blocking collectives: 30.7 us -> none  [per_device(): lax.all_gather(packed[1], 'blk', axis=0, tiled=True)]
    all_to_all x0 -> x1, starting transfers between devices: none -> 6.15 us  [per_device(): lax.all_to_all(jnp.stack([packed[1]] * lax.axis_size('blk')), 'blk', 0, 0)]
    sub x8, other arithmetic: 2.99 us -> 0.33 us  [attend(): query_pos[:, None] - span]
    ppermute x2, starting transfers between devices: 7.7 us -> 5.8 us  [from_behind(): return lax.ppermute(block, axis, route)]
    all_gather x1, blocking collectives: 7.48 us -> 9.11 us  [per_device(): lax.all_gather(values, 'grp', axis=0, tiled=True)]
  transfers between devices with their start and end apart: 3 -> 4, of which waited for: 0 -> 1; matrix products, arithmetic and copies ran while one was open for 20% -> 28% of each run, Pallas kernels for 0% -> 0%
where the time goes in v1:
time: 145 us; the launch traced here: 144 us
  blocking collectives  49.3 us (34%)
  local copies, waits for them, and re-layouts  32.4 us (22%)
  other arithmetic  23 us (16%)
  matrix products  18.6 us (13%)
  starting transfers between devices  16.5 us (11%)
  loops' own time  2.87 us (2%)
    all_gather x1, blocking collectives, per_device(): lax.all_gather(packed[0], 'blk', axis=0, tiled=True)  31.9 us
    all_gather x1, blocking collectives, per_device(): lax.all_gather(values, 'grp', axis=0, tiled=True)  9.11 us
    all_gather x1, blocking collectives, per_device(): lax.all_gather(keys, 'grp', axis=0, tiled=True)  8.24 us
    all_to_all x1, starting transfers between devices, per_device(): lax.all_to_all(jnp.stack([packed[1]] * lax.axis_size('blk')), 'blk', 0, 0)  6.15 us
    ppermute x2, starting transfers between devices, from_behind(): return lax.ppermute(block, axis, route)  5.8 us
    dynamic_update_slice x4, local copies, waits for them, and re-layouts, per_device(): fine, local = lax.map(both_blocks, jnp.arange(steps, dtype=jnp.int32))  4.59 us
    all_to_all x1, starting transfers between devices, per_device(): lax.all_to_all(outgoing, 'blk', split_axis=0, concat_axis=0, tiled=True)  4.55 us
    dot_general x8, matrix products, attend(): jnp.einsum('qhd,kd->qhk', query_rows, key_rows, preferred_element_type=jn...  4.55 us
  transfers between devices with their start and end apart: 4, of which 1 were waited for; matrix products, arithmetic and copies ran while one was open for 28% of the time, Pallas kernels for 0%

profile of v1, /device:TPU:0, one launch (start us, length us, event | category | flops | bytes accessed | tf_op | source)
XLA Modules:
  0.0 144.2 jit_solution(11631161596228009814)
XLA Ops:
  0.0 3.2 %collective-permute-start.1 = (bf16[512,128]{1,0:T(8,128)(2,1)}, bf16[512,128]{1,0:T(8,128)(2,1)}, u32[]{:S(2)}, u32[]{:S(2)}) collective-permute-start(bf16[512,128]{1,0:T(8,128)(2,1)} %param.14), channel_id=1, source_target_pairs={{0,1},{1,2},{2,3},{3,4},{4,5},{5,6},{6,7},{7,8},{8,9},{9,10},{10,1... | collective-permute-start | bytes 393224 | tf_op jit(solution)/shard_map/ppermute | solution.py:18
  3.2 9.1 %all_gather.11 = bf16[2048,128]{1,0:T(8,128)(2,1)S(1)} all-gather(bf16[512,128]{1,0:T(8,128)(2,1)} %param.14), channel_id=1, replica_groups=mesh['blk'=8,'grp'=4] {'grp'}, dimensions={0}, use_global_device_ids=true | all-gather | bytes 655360 | tf_op jit(solution)/shard_map/all_gather | solution.py:120
  13.0 1.2 reshape.491
  14.2 1.8 %convolution_convert_fusion = bf16[64,128]{1,0:T(8,128)(2,1)S(1)} fusion(bf16[256,128]{1,0:T(8,128)(2,1)S(1)} %copy-done.10, bf16[4096,256]{1,0:T(8,128)(2,1)S(1)} %copy-done, f32[64,4096]{1,0:T(8,128)} %reshape.491, f32[4096]{0:T(1024)S(1)} %get-tuple-element.393), kind=kOutput, calls=%fused_computation.57 | convolution fusion | flops 139026432 | bytes 3244032 | tf_op jit(solution)/shard_map/dot_general | solution.py:31
  16.7 6.2 %all-to-all-start = ((bf16[8,64,128]{2,1,0:T(8,128)(2,1)}), bf16[8,64,128]{2,1,0:T(8,128)(2,1)S(1)}, u32[]{:S(2)}, u32[]{:S(2)}) async-start(bf16[8,64,128]{2,1,0:T(8,128)(2,1)} %stack.2), calls=%async_computation | async-start | bytes 262144 | tf_op jit(solution)/shard_map/all_to_all | solution.py:137
  22.8 2.6 %collective-permute-start = (bf16[512,128]{1,0:T(8,128)(2,1)S(1)}, bf16[512,128]{1,0:T(8,128)(2,1)}, u32[]{:S(2)}, u32[]{:S(2)}) collective-permute-start(bf16[512,128]{1,0:T(8,128)(2,1)S(1)} %copy-done.6), channel_id=1, source_target_pairs={{0,1},{1,2},{2,3},{3,4},{4,5},{5,6},{6,7},{7,8},{8,9},{9,10},{10,1... | collective-permute-start | bytes 393224 | tf_op jit(solution)/shard_map/ppermute | solution.py:18
  25.5 8.2 %all_gather.9 = bf16[2048,128]{1,0:T(8,128)(2,1)S(1)} all-gather(bf16[512,128]{1,0:T(8,128)(2,1)S(1)} %copy-done.6), channel_id=1, replica_groups=mesh['blk'=8,'grp'=4] {'grp'}, dimensions={0}, use_global_device_ids=true | all-gather | bytes 655360 | tf_op jit(solution)/shard_map/all_gather | solution.py:119
  33.7 1.2 reshape.488
  34.9 1.1 pad_maximum_fusion
  39.3 2.5 %convolution_convert_fusion.1 = bf16[64,128]{1,0:T(8,128)(2,1)S(1)} fusion(bf16[256,128]{1,0:T(8,128)(2,1)S(1)} %copy-done.11, bf16[4096,256]{1,0:T(8,128)(2,1)} %param.16, f32[64,4096]{1,0:T(8,128)} %reshape.488, f32[4096]{0:T(1024)S(1)} %get-tuple-element.392), kind=kOutput, calls=%fused_computation.58 | convolution fusion | flops 139026432 | bytes 3244032 | tf_op jit(solution)/shard_map/dot_general | solution.py:31
  41.8 31.9 %all_gather.10 = bf16[512,128]{1,0:T(8,128)(2,1)S(1)} all-gather(bf16[64,128]{1,0:T(8,128)(2,1)S(1)} %convolution_convert_fusion.1), channel_id=1, replica_groups=mesh['blk'=8,'grp'=4] {'blk'}, dimensions={0}, use_global_device_ids=true | all-gather | bytes 147456 | tf_op jit(solution)/shard_map/all_gather | solution.py:135
  79.1 1.8 %gather_fusion.1 = bf16[8,64,256]{2,1,0:T(8,128)(2,1)S(1)} fusion(bf16[32,64,256]{2,1,0:T(8,128)(2,1)} %bitcast.142, s32[1024]{0:T(1024)S(1)} %pad_clamp_fusion.1), kind=kCustom, calls=%fused_computation.1 | custom fusion | bytes 524320 | tf_op jit(solution)/shard_map/jit(_take)/gather | solution.py:151
  80.9 1.4 broadcast_select_fusion
  82.3 1.3 pad_clamp_fusion
  83.6 2.6 %gather_fusion = bf16[16,64,256]{2,1,0:T(8,128)(2,1)} fusion(bf16[32,64,256]{2,1,0:T(8,128)(2,1)} %bitcast.143, s32[1024]{0:T(1024)S(1)} %get-tuple-element.402), kind=kCustom, calls=%fused_computation | custom fusion | bytes 1048640 | tf_op jit(solution)/shard_map/jit(_take)/gather | solution.py:155
  90.3 1.6 %copy.22 = f32[512,4]{1,0:T(8,128)} copy(f32[512,4]{0,1:T(4,128)} %get-tuple-element.389) | data formatting | bytes 16384 | tf_op jit(solution)/shard_map/mul | solution.py:194
  91.9 1.6 %copy.27 = f32[512,4]{1,0:T(8,128)} copy(f32[512,4]{0,1:T(4,128)} %get-tuple-element.390) | data formatting | bytes 16384 | tf_op jit(solution)/shard_map/mul | solution.py:194
  94.5 1.6 %pad_maximum_fusion.2 = bf16[1024,128]{1,0:T(8,128)(2,1)} fusion(bf16[512,128]{1,0:T(8,128)(2,1)S(1)} %copy-done.7, bf16[512,128]{1,0:T(8,128)(2,1)} %collective-permute-done.1), kind=kLoop, calls=%fused_computation.77 | loop fusion | flops 524288 | bytes 524288 | tf_op jit(solution)/shard_map/concatenate | solution.py:170
  96.1 4.6 %all-to-all-start.1 = ((bf16[8,64,256]{2,1,0:T(8,128)(2,1)}), bf16[8,64,256]{2,1,0:T(8,128)(2,1)S(1)}, u32[]{:S(2)}, u32[]{:S(2)}) async-start(bf16[8,64,256]{2,1,0:T(8,128)(2,1)} %broadcast_select_fusion), calls=%async_computation.1 | async-start | bytes 524288 | tf_op jit(solution)/shard_map/all_to_all | solution.py:152
  100.6 4.4 %divide_multiply_fusion = f32[512,4,128]{0,2,1:T(8,128)} fusion(bf16[512,128,1]{1,0,2:T(8,128)(2,1)S(1)} %bitcast.147, f32[512,512,4]{1,0,2:T(8,128)} %copy-done.1, f32[512,4]{0,1:T(4,128)S(1)} %broadcast_maximum_fusion, pred[512,512]{0,1:T(8,128)(4,1)S(1)} %broadcast_compare_fusion.2, f32[512,4]{0,1:T(4,128)} %get-tuple-element.395, ...), kind=kOutput, calls=%fused_computation.65 | convolution fusion | flops 273416192 | bytes 5668864 | tf_op jit(solution)/shard_map/while/body/eval_jaxpr/qhk,kd->qhd/dot_general | solution.py:81
  105.0 2.5 %copy.26 = f32[512,512]{1,0:T(8,128)} copy(f32[512,512]{0,1:T(8,128)} %bitcast.144) | data formatting | bytes 2097152 | tf_op jit(solution)/shard_map/mul | solution.py:194
  107.5 1.3 all-to-all-done.1
  108.9 1.5 %gather_fusion.2 = bf16[16,64,256]{2,1,0:T(8,128)(2,1)} fusion(bf16[8,64,256]{2,1,0:T(8,128)(2,1)S(1)} %all-to-all-done.1, s32[1024]{0:T(1024)} %get-tuple-element.401), kind=kCustom, calls=%fused_computation.2 | custom fusion | bytes 1048640 | tf_op jit(solution)/shard_map/jit(_take)/gather | solution.py:156
  110.4 1.9 %fusion.49 = bf16[1024,256]{1,0:T(8,128)(2,1)S(1)} fusion(bf16[16,64,256]{2,1,0:T(8,128)(2,1)} %gather_fusion.2, bf16[16,64,256]{2,1,0:T(8,128)(2,1)} %gather_fusion, pred[1024]{0:T(1024)(128)(4,1)S(1)} %copy-done.15, pred[1024]{0:T(1024)(128)(4,1)S(1)} %copy-done.17, pred[1024]{0:T(1024)(128)(4,1)S(1)} %copy-done.16), kind=kLoop, calls=%fused_computation.71 | loop fusion | flops 786432 | bytes 1575936 | tf_op jit(solution)/shard_map/jit(_where)/select_n | solution.py:157
  113.0 25.4 %while.24 = (s32[]{:T(128)}, f32[4,128,4,128]{3,2,1,0:T(4,128)}, f32[4,128,4,128]{3,2,1,0:T(4,128)}, s32[4]{0:T(128)S(1)}, s32[512]{0:T(512)S(1)}, /*index=5*/bf...) while((s32[]{:T(128)}, f32[4,128,4,128]{3,2,1,0:T(4,128)}, ...), condition=%wide.region_8.9_spmd.clone, body=%wide.region_3.8_spmd.clone.sunk | while | flops 445252480 | bytes 15753344 | solution.py:187
  118.2 1.1 copy_dynamic-update-slice_fusion.3
  124.5 1.1 copy_dynamic-update-slice_fusion.3
  130.9 1.1 copy_dynamic-update-slice_fusion.3
  137.2 1.2 copy_dynamic-update-slice_fusion.3
  138.4 1.7 %mul.142 = f32[512,4,128]{2,1,0:T(4,128)S(1)} broadcast(f32[512,4]{1,0:T(8,128)} %copy.22), dimensions={0,1} | broadcast | bytes 1056768 | tf_op jit(solution)/shard_map/mul | solution.py:194
  140.1 1.6 %mul.147 = f32[512,4,128]{2,1,0:T(4,128)S(1)} broadcast(f32[512,4]{1,0:T(8,128)} %copy.27), dimensions={0,1} | broadcast | bytes 1056768 | tf_op jit(solution)/shard_map/mul | solution.py:194
  141.7 2.5 %fusion.43 = bf16[512,512]{1,0:T(8,128)(2,1)} fusion(f32[64,8,4,128]{3,2,1,0:T(4,128)} %bitcast.146, f32[64,8,4,128]{3,2,1,0:T(4,128)S(1)} %bitcast.141, f32[512,512]{1,0:T(8,128)S(1)} %copy-done.2, f32[64,8,4,128]{3,2,1,0:T(4,128)S(1)} %bitcast.145, f32[64,8,4,128]{3,2,1,0:T(4,128)S(1)} %bitcast.140), kind=kLoop, calls=%fused_computation.61 | loop fusion | flops 1310720 | bytes 5767168 | tf_op jit(solution)/shard_map/convert_element_type | solution.py:196
  (152 shorter events, 33.8 us)
Async XLA Ops:
  0.0 14.2 %copy-start = (bf16[4096,256]{1,0:T(8,128)(2,1)S(1)}, bf16[4096,256]{1,0:T(8,128)(2,1)}, u32[]{:S(2)}) copy-start(bf16[4096,256]{1,0:T(8,128)(2,1)} %param.18) | copy-start | bytes 6291460
  0.0 14.2 %copy-start.10 = (bf16[256,128]{1,0:T(8,128)(2,1)S(1)}, bf16[256,128]{1,0:T(8,128)(2,1)}, u32[]{:S(2)}) copy-start(bf16[256,128]{1,0:T(8,128)(2,1)} %param.19) | copy-start | bytes 196612
  0.0 94.4 %collective-permute-start.1 = (bf16[512,128]{1,0:T(8,128)(2,1)}, bf16[512,128]{1,0:T(8,128)(2,1)}, u32[]{:S(2)}, u32[]{:S(2)}) collective-permute-start(bf16[512,128]{1,0:T(8,128)(2,1)} %param.14), channel_id=1, source_target_pairs={{0,1},{1,2},{2,3},{3,4},{4,5},{5,6},{6,7},{7,8},{8,9},{9,10},{10,1... | collective-permute-start | bytes 393224 | tf_op jit(solution)/shard_map/ppermute | solution.py:18
  14.2 8.6 %copy-start.6 = (bf16[512,128]{1,0:T(8,128)(2,1)S(1)}, bf16[512,128]{1,0:T(8,128)(2,1)}, u32[]{:S(2)}) copy-start(bf16[512,128]{1,0:T(8,128)(2,1)} %param.13) | copy-start | bytes 393220
  16.7 79.4 %all-to-all-start = ((bf16[8,64,128]{2,1,0:T(8,128)(2,1)}), bf16[8,64,128]{2,1,0:T(8,128)(2,1)S(1)}, u32[]{:S(2)}, u32[]{:S(2)}) async-start(bf16[8,64,128]{2,1,0:T(8,128)(2,1)} %stack.2), calls=%async_computation | async-start | bytes 262144 | tf_op jit(solution)/shard_map/all_to_all | solution.py:137
  22.8 70.7 %collective-permute-start = (bf16[512,128]{1,0:T(8,128)(2,1)S(1)}, bf16[512,128]{1,0:T(8,128)(2,1)}, u32[]{:S(2)}, u32[]{:S(2)}) collective-permute-start(bf16[512,128]{1,0:T(8,128)(2,1)S(1)} %copy-done.6), channel_id=1, source_target_pairs={{0,1},{1,2},{2,3},{3,4},{4,5},{5,6},{6,7},{7,8},{8,9},{9,10},{10,1... | collective-permute-start | bytes 393224 | tf_op jit(solution)/shard_map/ppermute | solution.py:18
  25.5 10.6 %copy-start.12 = (s32[32,16]{0,1:T(8,128)S(1)}, s32[32,16]{0,1:T(8,128)}, u32[]{:S(2)}) copy-start(s32[32,16]{0,1:T(8,128)} %param.15) | copy-start | bytes 6148
  25.5 13.8 %copy-start.11 = (bf16[256,128]{1,0:T(8,128)(2,1)S(1)}, bf16[256,128]{1,0:T(8,128)(2,1)}, u32[]{:S(2)}) copy-start(bf16[256,128]{1,0:T(8,128)(2,1)} %param.17) | copy-start | bytes 196612
  36.0 37.7 %copy-start.3 = (bf16[512,512]{1,0:T(8,128)(2,1)S(1)}, bf16[512,512]{1,0:T(8,128)(2,1)}, u32[]{:S(2)}) copy-start(bf16[512,512]{1,0:T(8,128)(2,1)} %param.12) | copy-start | bytes 1572868
  75.0 2.0 %copy-start.1 = (f32[512,512,4]{1,0,2:T(8,128)}, f32[512,512,4]{1,0,2:T(8,128)S(1)}, u32[]{:S(2)}) copy-start(f32[512,512,4]{1,0,2:T(8,128)S(1)} %get-tuple-element.400) | copy-start | bytes 12582916
  75.0 2.6 %copy-start.4 = (bf16[512,512]{1,0:T(8,128)(2,1)S(1)}, bf16[512,512]{1,0:T(8,128)(2,1)}, u32[]{:S(2)}) copy-start(bf16[512,512]{1,0:T(8,128)(2,1)} %param.12) | copy-start | bytes 1572868
  75.1 2.6 %copy-start.13 = (bf16[512,12]{0,1:T(8,128)(2,1)S(1)}, bf16[512,12]{0,1:T(8,128)(2,1)}, u32[]{:S(2)}) copy-start(bf16[512,12]{0,1:T(8,128)(2,1)} %param.21) | copy-start | bytes 36868
  75.1 3.4 %copy-start.18 = (s32[8]{0:T(128)S(1)}, s32[8]{0:T(128)}, u32[]{:S(2)}) copy-start(s32[8]{0:T(128)} %fusion.63) | copy-start | bytes 100
  75.1 3.4 %copy-start.19 = (s32[16]{0:T(128)S(1)}, s32[16]{0:T(128)}, u32[]{:S(2)}) copy-start(s32[16]{0:T(128)} %get-tuple-element.380) | copy-start | bytes 196
  77.0 17.5 %copy-start.7 = (bf16[512,128]{1,0:T(8,128)(2,1)S(1)}, bf16[512,128]{1,0:T(8,128)(2,1)}, u32[]{:S(2)}) copy-start(bf16[512,128]{1,0:T(8,128)(2,1)} %param.14) | copy-start | bytes 393220
  96.1 12.8 %all-to-all-start.1 = ((bf16[8,64,256]{2,1,0:T(8,128)(2,1)}), bf16[8,64,256]{2,1,0:T(8,128)(2,1)S(1)}, u32[]{:S(2)}, u32[]{:S(2)}) async-start(bf16[8,64,256]{2,1,0:T(8,128)(2,1)} %broadcast_select_fusion), calls=%async_computation.1 | async-start | bytes 524288 | tf_op jit(solution)/shard_map/all_to_all | solution.py:152
  105.0 5.4 %copy-start.15 = (pred[1024]{0:T(1024)(128)(4,1)S(1)}, pred[1024]{0:T(1024)(128)(4,1)}, u32[]{:S(2)}) copy-start(pred[1024]{0:T(1024)(128)(4,1)} %broadcast_in_dim.198) | copy-start | bytes 3076
  105.0 5.4 %copy-start.16 = (pred[1024]{0:T(1024)(128)(4,1)S(1)}, pred[1024]{0:T(1024)(128)(4,1)}, u32[]{:S(2)}) copy-start(pred[1024]{0:T(1024)(128)(4,1)} %broadcast_in_dim.191) | copy-start | bytes 3076
  105.0 5.4 %copy-start.17 = (pred[1024]{0:T(1024)(128)(4,1)S(1)}, pred[1024]{0:T(1024)(128)(4,1)}, u32[]{:S(2)}) copy-start(pred[1024]{0:T(1024)(128)(4,1)} %broadcast_in_dim.194) | copy-start | bytes 3076
  107.5 5.5 %copy-start.14 = (s32[16]{0:T(128)S(1)}, s32[16]{0:T(128)}, u32[]{:S(2)}) copy-start(s32[16]{0:T(128)} %broadcast_multiply_fusion) | copy-start | bytes 196
  114.7 1.2 copy-start.9
  116.6 1.1 copy-start.8
  121.1 1.2 copy-start.9
  123.0 1.1 copy-start.8
  127.4 1.2 copy-start.9
  129.3 1.1 copy-start.8
  133.7 1.2 copy-start.9
  135.7 1.1 copy-start.8
  138.4 3.3 %copy-start.2 = (f32[512,512]{1,0:T(8,128)S(1)}, f32[512,512]{1,0:T(8,128)}, u32[]{:S(2)}) copy-start(f32[512,512]{1,0:T(8,128)} %copy.26) | copy-start | bytes 3145732
  138.4 3.3 %copy-start.5 = (f32[4,128,4,128]{3,2,1,0:T(4,128)S(1)}, f32[4,128,4,128]{3,2,1,0:T(4,128)}, u32[]{:S(2)}) copy-start(f32[4,128,4,128]{3,2,1,0:T(4,128)} %get-tuple-element.299) | copy-start | bytes 3145732
